TPU v7x, 32 devices: a whole 2x2x4 slice. The times are simulated.
32 devices in a mesh: dp: 4 (over z), frame: 2 (over x), audio: 4 (over y, core).
Axes of the slice: x: 2, y: 2, z: 4, core: 2. Of those that a mesh axis runs over, the one named last changes fastest.
Arguments:
- video_query: bfloat16 [4, 1024, 3072], P('dp', ('frame', 'audio')), may hold values from -72 to 72
- out_grad: bfloat16 [4, 1024, 3072], P('dp', ('frame', 'audio')), may hold values from -6 to 6
- audio_latents: bfloat16 [4, 1024, 3072], P('dp', 'audio'), may hold values from -6 to 6
- kv_weight: bfloat16 [3072, 2, 3072], P(None, None, 'frame'), may hold values from -0.4375 to 0.4375
- video_length: int32 [4], P('dp'), may hold values from 256 to 1024, as said below
- audio_length: int32 [4], P('dp'), may hold values from 128 to 1024, as said below
- align_list: int32 [4, 8, 2], P('dp'), may hold values from 0 to 15, as said below
Outputs:
- attended: bfloat16 [4, 1024, 3072], P('dp', ('frame', 'audio'))
- query_grad: bfloat16 [4, 1024, 3072], P('dp', ('frame', 'audio'))
- kv_weight_grad: float32 [3072, 2, 3072], P(('dp', 'audio'), None, 'frame')
Inputs may be any that keep to these rules, and one draw needn't show every extreme that they name: `video_length`: one clip of every draw has all 1024 tokens live. `audio_length`: one clip of every draw has all 1024 latents live. `align_list`: for clip c and query block b the 2 entries are distinct and each is below ceil(audio_length[c] / 64); the first is b * ceil(audio_length[c] / 64) // 8.
All inputs are finite; a program needn't handle non-finite values.
Results may differ from a plain program's by a relative error of at most 0.004.
The roundings to bfloat16 on the way count: a program that leaves them out, or rounds other values in their place, can miss the bound.
Values may be sent and summed in bfloat16 or wider, within the bound.
A program may use at most 192 MiB of HBM per device.

v0:
```python
import math

import jax
import jax.numpy as jnp
from jax import lax
from jax.sharding import PartitionSpec as P

D = 3072
HD = 128
QB = 128
KB = 64


def softmax_core(query_rows, grad_rows, key_rows, value_rows, allowed, live_rows):
    scaling = HD ** (-0.5)
    scores = (
        jnp.einsum("bqhd,bkhd->bhqk", query_rows, key_rows, preferred_element_type=jnp.float32)
        * scaling
    )
    scores = jnp.where(allowed[:, None], scores, -1e30)
    scores = scores - jnp.max(scores, axis=-1, keepdims=True)
    weights = jnp.exp(scores)
    probability = weights / jnp.sum(weights, axis=-1, keepdims=True)
    probability = jnp.where(live_rows[:, None, :, None], probability, 0.0)
    prob_low = probability.astype(jnp.bfloat16)
    output = jnp.einsum(
        "bhqk,bkhd->bqhd", prob_low, value_rows, preferred_element_type=jnp.float32
    ).astype(jnp.bfloat16)
    prob_grad = jnp.einsum(
        "bqhd,bkhd->bhqk", grad_rows, value_rows, preferred_element_type=jnp.float32
    )
    row_dot = jnp.sum(probability * prob_grad, axis=-1, keepdims=True)
    score_grad = (probability * (prob_grad - row_dot)).astype(jnp.bfloat16)
    query_part = (
        jnp.einsum("bhqk,bkhd->bqhd", score_grad, key_rows, preferred_element_type=jnp.float32)
        * scaling
    )
    key_part = (
        jnp.einsum("bhqk,bqhd->bkhd", score_grad, query_rows, preferred_element_type=jnp.float32)
        * scaling
    )
    value_part = jnp.einsum(
        "bhqk,bqhd->bkhd", prob_low, grad_rows, preferred_element_type=jnp.float32
    )
    return (output, query_part.astype(jnp.bfloat16), jnp.stack([key_part, value_part], axis=2))


def attend_masked(
    queries, cotangent, positions, key_table, block_lists, video_live, audio_live, heads
):
    row_total = queries.shape[0]
    key_count = key_table.shape[0]
    block_count = key_count // KB
    head_width = heads * HD
    step_rows = math.gcd(row_total, 512)
    step_count = row_total // step_rows
    kv_table = key_table.reshape(1, key_count, 2, heads, HD)
    key_live = jnp.arange(key_count) < audio_live
    block_ids = jnp.arange(block_count)

    def advance(totals, inputs):
        query_rows, grad_rows, row_index = inputs
        listed = block_lists[row_index // QB]
        allowed_blocks = jnp.any(listed[:, :, None] == block_ids[None, None, :], axis=1)
        allowed = jnp.repeat(allowed_blocks, KB, axis=1) & key_live[None, :]
        output, query_part, grad_part = softmax_core(
            query_rows[None],
            grad_rows[None],
            kv_table[:, :, 0],
            kv_table[:, :, 1],
            allowed[None],
            (row_index < video_live)[None],
        )
        return (totals + grad_part[0], (output[0], query_part[0]))

    totals = jnp.zeros((key_count, 2, heads, HD), jnp.float32)
    shaped = (
        queries.reshape(step_count, step_rows, heads, HD),
        cotangent.reshape(step_count, step_rows, heads, HD),
        positions.reshape(step_count, step_rows),
    )
    totals, (output, query_part) = lax.scan(advance, totals, shaped)
    return (
        output.reshape(row_total, head_width),
        query_part.reshape(row_total, head_width),
        totals.reshape(key_count, 2 * head_width),
    )


def attend(queries, cotangent, positions, key_table, block_lists, video_live, audio_live, heads):
    return attend_masked(
        queries, cotangent, positions, key_table, block_lists, video_live, audio_live, heads
    )


def per_device(
    video_query, out_grad, audio_latents, kv_weight, video_length, audio_length, align_list
):
    frames = lax.axis_size("frame")
    audio_count = lax.axis_size("audio")
    audio_at = lax.axis_index("audio")
    queries = video_query[0]
    cotangent = out_grad[0]
    latents = audio_latents[0]
    shard_rows = queries.shape[0]
    local_width = kv_weight.shape[2]
    video_live = video_length[0]
    audio_live = audio_length[0]
    block_lists = align_list[0]
    projected = jnp.dot(
        latents, kv_weight.reshape(D, 2 * local_width), preferred_element_type=jnp.float32
    ).astype(jnp.bfloat16)
    head_queries, head_cotangent = (
        lax.all_to_all(queries, "frame", split_axis=1, concat_axis=0, tiled=True),
        lax.all_to_all(cotangent, "frame", split_axis=1, concat_axis=0, tiled=True),
    )
    key_table = lax.all_gather(projected, "audio", axis=0, tiled=True)
    source = jnp.arange(frames * shard_rows) // shard_rows
    offset = jnp.arange(frames * shard_rows) % shard_rows
    positions = (source * audio_count + audio_at) * shard_rows + offset
    attended, query_grad, key_part = attend(
        head_queries,
        head_cotangent,
        positions,
        key_table,
        block_lists,
        video_live,
        audio_live,
        local_width // HD,
    )
    attended, query_grad = (
        lax.all_to_all(attended, "frame", split_axis=0, concat_axis=1, tiled=True),
        lax.all_to_all(query_grad, "frame", split_axis=0, concat_axis=1, tiled=True),
    )
    key_grad = lax.psum_scatter(key_part, "audio", scatter_dimension=0, tiled=True)
    key_grad = key_grad.astype(jnp.bfloat16)
    clip_count = lax.axis_size("dp")
    weight_rows = D // (clip_count * audio_count)
    product = lax.dot_general(
        latents, key_grad, (((0,), (0,)), ((), ())), preferred_element_type=jnp.float32
    )
    weight_grad = lax.psum_scatter(
        product * (1.0 / clip_count), ("dp", "audio"), scatter_dimension=0, tiled=True
    )
    return (attended[None], query_grad[None], weight_grad.reshape(weight_rows, 2, local_width))


def solution(mesh):
    return jax.shard_map(
        per_device,
        mesh=mesh,
        in_specs=(
            P("dp", ("frame", "audio"), None),
            P("dp", ("frame", "audio"), None),
            P("dp", "audio", None),
            P(None, None, "frame"),
            P("dp"),
            P("dp"),
            P("dp", None, None),
        ),
        out_specs=(
            P("dp", ("frame", "audio"), None),
            P("dp", ("frame", "audio"), None),
            P(("dp", "audio"), None, "frame"),
        ),
        check_vma=False,
    )
```

profile of v0, /device:TPU:0, one launch (start us, length us, event | category | flops | bytes accessed | tf_op | source)
XLA Modules:
  0.0 683.0 jit_solution(10944515111955823411)
XLA Ops:
  7.2 0.0 all-gather.2.cloned.1.call-start
  7.2 12.9 %copy.92 = bf16[384,8,2,1536]{3,1,2,0:T(8,128)(2,1)S(1)} copy(bf16[384,8,2,1536]{3,2,1,0:T(2,128)(2,1)} %bitcast.115) | data formatting | bytes 37748736
  20.2 6.3 convolution_convert_fusion
  26.5 0.0 all-gather.2.cloned.1.call-update
  26.5 1.2 copy.64
  27.7 4.2 all-to-all-start
  33.2 0.1 copy.61
  33.3 1.2 copy.69
  34.5 9.0 %all-to-all-done = bf16[128,2,1536]{0,2,1:T(8,128)(2,1)S(1)} async-done(((bf16[128,2,1536]{0,2,1:T(8,128)(2,1)}), bf16[128,2,1536]{0,2,1:T(8,128)(2,1)S(1)}, u32[]{:S(2)}, u32[]{:S(2)}) %all-to-all-start) | async-done | bytes 786464 | tf_op jit(solution)/shard_map/all_to_all | solution.py:114
  43.5 3.6 all-to-all-start.2
  47.1 0.0 reduce-scatter.5.cloned.1.call-start
  47.2 0.7 gather_fusion
  47.9 0.1 copy.62
  48.0 0.2 bitcast_and_fusion
  48.2 7.4 %copy.65 = bf16[2,128,1536]{1,0,2:T(2,128)(2,1)} copy(bf16[2,128,1536]{1,2,0:T(8,128)(2,1)S(1)} %bitcast.124) | data formatting | bytes 1572864 | tf_op jit(solution)/shard_map/all_to_all | solution.py:114
  55.7 2.4 reshape.300
  58.1 7.3 %copy.70 = bf16[2,128,1536]{1,0,2:T(2,128)(2,1)} copy(bf16[2,128,1536]{1,2,0:T(8,128)(2,1)S(1)} %bitcast.125) | data formatting | bytes 1572864 | tf_op jit(solution)/shard_map/all_to_all | solution.py:115
  65.4 2.4 reshape.301
  67.8 8.0 %all-gather.2.cloned.1.call-done = bf16[1024,3072]{1,0:T(8,128)(2,1)} async-done(((bf16[256,3072]{1,0:T(8,128)(2,1)}), bf16[1024,3072]{1,0:T(8,128)(2,1)}) %all-gather.2.cloned.1.call-update) | async-done | bytes 6291472 | tf_op jit(solution)/shard_map/all_gather | solution.py:117
  75.8 8.6 %copy.60 = bf16[1024,3072]{0,1:T(8,128)(2,1)} copy(bf16[1024,3072]{1,0:T(8,128)(2,1)} %all-gather.2.cloned.1.call-done) | data formatting | bytes 12582912 | tf_op jit(solution)/shard_map/all_gather | solution.py:117
  84.4 8.3 %fusion.14 = f32[12,1024,256]{2,1,0:T(8,128)} fusion(bf16[256,12,128]{0,2,1:T(8,128)(2,1)S(1)} %reshape.300, bf16[1,1024,2,12,128]{1,4,3,2,0:T(8,128)(2,1)} %bitcast.117), kind=kOutput, calls=%fused_computation.26 | convolution fusion | flops 805306368 | bytes 16515072 | tf_op jit(solution)/shard_map/while/body/eval_jaxpr/bqhd,bkhd->bhqk/dot_general | solution.py:17
  92.6 13.7 %fusion.42 = (f32[12,256]{1,0:T(8,128)S(1)}, f32[12,256,1024]{1,2,0:T(8,128)}) fusion(f32[12,1024,256]{2,1,0:T(8,128)} %fusion.14, pred[256,1024]{0,1:T(8,128)(4,1)S(1)} %bitcast_and_fusion), kind=kOutput, calls=%fused_computation.68 | output fusion | flops 18875392 | bytes 25440256 | tf_op jit(solution)/shard_map/while/body/eval_jaxpr/sub | solution.py:21
  106.3 9.5 %fusion.15 = f32[1,1024,1,12,128]{1,4,3,2,0:T(8,128)} fusion(bf16[256,12,128]{0,2,1:T(8,128)(2,1)S(1)} %reshape.301, f32[12,256,1024]{1,2,0:T(8,128)} %get-tuple-element.52, f32[12,256]{1,0:T(8,128)S(1)} %get-tuple-element.51, pred[256]{0:T(512)(128)(4,1)S(1)} %fusion.36), kind=kOutput, calls=%fused_computation.27 | convolution fusion | flops 814743552 | bytes 19673344 | tf_op jit(solution)/shard_map/while/body/eval_jaxpr/bhqk,bqhd->bkhd/dot_general | solution.py:42
  115.8 8.6 %fusion.1 = (f32[12,256]{1,0:T(8,128)S(1)}, f32[12,1024,256]{2,1,0:T(8,128)}) fusion(f32[12,256,1024]{1,2,0:T(8,128)} %get-tuple-element.52, f32[12,256]{1,0:T(8,128)S(1)} %get-tuple-element.51, pred[256]{0:T(512)(128)(4,1)S(1)} %fusion.36, bf16[256,12,128]{0,2,1:T(8,128)(2,1)S(1)} %reshape.301, bf16[1,1024,2,12,128]{1,4,3,2,0:T(8,128)(2,1)S(1)} %bitcast.122), kind=kOutput, calls=%fused_computation.6 | convolution fusion | flops 817886208 | bytes 29127168 | tf_op jit(solution)/shard_map/while/body/eval_jaxpr/bqhd,bkhd->bhqk/dot_general | solution.py:29
  124.5 9.2 %fusion.3 = bf16[12,256,1024]{1,2,0:T(8,128)(2,1)S(1)} fusion(f32[12,1024,256]{2,1,0:T(8,128)} %get-tuple-element.54, f32[12,256]{1,0:T(8,128)S(1)} %get-tuple-element.53, f32[12,256,1024]{1,2,0:T(8,128)} %get-tuple-element.52, f32[12,256]{1,0:T(8,128)S(1)} %get-tuple-element.51, pred[256]{0:T(512)(128)(4,1)S(1)} %fusion.36), kind=kLoop, calls=%fused_computation.8 | loop fusion | flops 15728640 | bytes 31482112 | tf_op jit(solution)/shard_map/while/body/eval_jaxpr/convert_element_type | solution.py:33
  133.7 2.7 copy-done.2
  136.3 4.8 multiply_bitcast_fusion.1
  141.1 11.9 %pad_maximum_fusion = f32[1,1024,2,12,128]{1,4,3,2,0:T(8,128)} fusion(f32[1,1024,1,12,128]{1,4,3,2,0:T(8,128)} %fusion.15, f32[1,1024,1,12,128]{1,4,3,2,0:T(8,128)} %multiply_bitcast_fusion.1), kind=kLoop, calls=%fused_computation.3 | loop fusion | flops 3145728 | bytes 25165824 | tf_op jit(solution)/shard_map/while/body/eval_jaxpr/stack | solution.py:45
  153.0 0.0 reduce-scatter.5.cloned.1.call-update
  153.0 0.0 reduce-scatter.7.cloned.1.call-start
  153.1 97.3 %reduce-scatter.5.cloned.1.call-done = f32[256,3072]{0,1:T(8,128)} async-done(((f32[1024,3072]{0,1:T(8,128)}), f32[256,3072]{0,1:T(8,128)}) %reduce-scatter.5.cloned.1.call-update) | async-done | bytes 3145744 | tf_op jit(solution)/shard_map/reduce_scatter | solution.py:135
  250.3 16.6 %multiply_bitcast_fusion = f32[3072,3072]{0,1:T(8,128)} fusion(bf16[1,256,3072]{2,1,0:T(8,128)(2,1)S(1)} %copy-done, f32[256,3072]{0,1:T(8,128)} %reduce-scatter.5.cloned.1.call-done), kind=kOutput, calls=%fused_computation.2 | convolution fusion | flops 4842061824 | bytes 42467328 | tf_op jit(solution)/shard_map/dot_general | solution.py:139
  267.0 36.9 %copy.89 = f32[3072,3072]{1,0:T(8,128)} copy(f32[3072,3072]{0,1:T(8,128)} %multiply_bitcast_fusion) | data formatting | bytes 75497472
  303.8 6.7 fusion.24
  310.5 0.2 all_to_all.51
  310.7 1.0 copy.68
  311.7 3.6 all-to-all-start.1
  315.3 6.6 fusion.27
  321.9 0.2 all_to_all.57
  322.1 1.0 copy.75
  323.1 3.1 all-to-all-done.1
  326.1 3.6 all-to-all-start.3
  329.7 1.2 copy.78
  330.9 8.9 %all-to-all-done.3 = bf16[2,128,1536]{1,2,0:T(8,128)(2,1)S(1)} async-done(((bf16[2,128,1536]{1,2,0:T(8,128)(2,1)}), bf16[2,128,1536]{1,2,0:T(8,128)(2,1)S(1)}, u32[]{:S(2)}, u32[]{:S(2)}) %all-to-all-start.3) | async-done | bytes 786464 | tf_op jit(solution)/shard_map/all_to_all | solution.py:133
  339.8 1.2 copy.79
  341.0 327.7 %reduce-scatter.7.cloned.1.call-done = f32[192,3072]{1,0:T(8,128)} async-done(((f32[3072,3072]{1,0:T(8,128)}), f32[192,3072]{1,0:T(8,128)}) %reduce-scatter.7.cloned.1.call-update) | async-done | bytes 2359312
  668.7 3.4 copy.90
  672.1 4.5 copy.80
  (23 shorter events, 0.1 us)
Async XLA Ops:
  7.2 12.9 %copy-start = (bf16[1,256,3072]{2,1,0:T(8,128)(2,1)S(1)}, bf16[1,256,3072]{2,1,0:T(8,128)(2,1)}, u32[]{:S(2)}) copy-start(bf16[1,256,3072]{2,1,0:T(8,128)(2,1)} %param.9) | copy-start | bytes 4718596
  7.2 68.6 %all-gather.2.cloned.1.call-start = ((), (), s32[]{:S(2)}) async-start(), calls=%async_computation.6 | async-start | bytes 7864320 | tf_op jit(solution)/shard_map/all_gather | solution.py:117
  20.1 6.4 copy-start.3
  20.1 13.1 %copy-start.5 = (s32[1,8,2]{1,2,0:T(2,128)S(1)}, s32[1,8,2]{1,2,0:T(2,128)}, u32[]{:S(2)}) copy-start(s32[1,8,2]{1,2,0:T(2,128)} %param.13) | copy-start | bytes 196
  20.1 13.2 %copy-start.4 = (bf16[1,128,3072]{2,1,0:T(8,128)(2,1)S(1)}, bf16[1,128,3072]{2,1,0:T(8,128)(2,1)}, u32[]{:S(2)}) copy-start(bf16[1,128,3072]{2,1,0:T(8,128)(2,1)} %param.8) | copy-start | bytes 2359300
  27.7 15.8 %all-to-all-start = ((bf16[128,2,1536]{0,2,1:T(8,128)(2,1)}), bf16[128,2,1536]{0,2,1:T(8,128)(2,1)S(1)}, u32[]{:S(2)}, u32[]{:S(2)}) async-start(bf16[128,2,1536]{0,2,1:T(8,128)(2,1)} %bitcast.9), calls=%async_computation | async-start | bytes 1572864 | tf_op jit(solution)/shard_map/all_to_all | solution.py:114
  43.5 14.6 %all-to-all-start.2 = ((bf16[128,2,1536]{0,2,1:T(8,128)(2,1)}), bf16[128,2,1536]{0,2,1:T(8,128)(2,1)S(1)}, u32[]{:S(2)}, u32[]{:S(2)}) async-start(bf16[128,2,1536]{0,2,1:T(8,128)(2,1)} %bitcast.16), calls=%async_computation.2 | async-start | bytes 1572864 | tf_op jit(solution)/shard_map/all_to_all | solution.py:115
  47.1 203.2 %reduce-scatter.5.cloned.1.call-start = ((), (), s32[]{:S(2)}) async-start(), calls=%async_computation.7 | async-start | bytes 15728640 | tf_op jit(solution)/shard_map/reduce_scatter | solution.py:135
  92.6 23.2 %slice-start = ((s8[6291456]{0:T(1024)(128)(4,1)}), s8[4194304]{0:T(1024)(128)(4,1)S(1)}, s32[]{:S(2)}) async-start(s8[6291456]{0:T(1024)(128)(4,1)} %bitcast.120), calls=%async_computation.9 | async-start | bytes 8388608
  106.3 9.5 %slice-start.1 = ((s8[6291456]{0:T(1024)(128)(4,1)}), s8[2097152]{0:T(1024)(128)(4,1)S(1)}, s32[]{:S(2)}) async-start(s8[6291456]{0:T(1024)(128)(4,1)} %bitcast.120), calls=%async_computation.10 | async-start | bytes 4194304
  133.6 2.7 copy-start.2
  153.0 515.6 %reduce-scatter.7.cloned.1.call-start = ((), (), s32[]{:S(2)}) async-start(), calls=%async_computation.8 | async-start | bytes 40108032
  311.7 14.5 %all-to-all-start.1 = ((bf16[2,128,1536]{1,2,0:T(8,128)(2,1)}), bf16[2,128,1536]{1,2,0:T(8,128)(2,1)S(1)}, u32[]{:S(2)}, u32[]{:S(2)}) async-start(bf16[2,128,1536]{1,2,0:T(8,128)(2,1)} %copy.68), calls=%async_computation.1 | async-start | bytes 1572864 | tf_op jit(solution)/shard_map/all_to_all | solution.py:132
  326.1 13.7 %all-to-all-start.3 = ((bf16[2,128,1536]{1,2,0:T(8,128)(2,1)}), bf16[2,128,1536]{1,2,0:T(8,128)(2,1)S(1)}, u32[]{:S(2)}, u32[]{:S(2)}) async-start(bf16[2,128,1536]{1,2,0:T(8,128)(2,1)} %copy.75), calls=%async_computation.3 | async-start | bytes 1572864 | tf_op jit(solution)/shard_map/all_to_all | solution.py:133
  339.8 336.7 %copy-start.1 = (bf16[1,256,3072]{2,1,0:T(8,128)(2,1)S(1)}, bf16[1,256,3072]{2,1,0:T(8,128)(2,1)}, u32[]{:S(2)}) copy-start(bf16[1,256,3072]{2,1,0:T(8,128)(2,1)} %param.9) | copy-start | bytes 4718596
Sparse Core Ops, SparseCore 0:
  26.7 49.0 all-gather.1
  153.1 97.1 reduce-scatter.4
  304.0 364.6 reduce-scatter.6
where the time goes:
time: 684 us; the launch traced here: 683 us
  waiting for transfers between devices  454 us (66%)
  local copies, waits for them, and re-layouts  96.3 us (14%)
  matrix products  67.5 us (10%)
  other arithmetic  35 us (5%)
  between operations  15.2 us (2%)
  starting transfers between devices  15.1 us (2%)
    unnamed x4, waiting for transfers between devices  328 us
    reduce_scatter x1, waiting for transfers between devices, per_device(): lax.psum_scatter(key_part, 'audio', scatter_dimension=0, tiled=True)  97.3 us
    unnamed x24, local copies, waits for them, and re-layouts  64.9 us
    dot_general x1, matrix products, per_device(): lax.dot_general(latents, key_grad, (((0,), (0,)), ((), ())), preferred_el...  16.6 us
  transfers between devices with their start and end apart: 7, of which 6 were waited for; matrix products, arithmetic and copies ran while one was open for 6% of the time, Pallas kernels for 0%

commit v1 on v0

v1 whole, which is shorter than its diff:
```python
import functools
import math

import jax
import jax.numpy as jnp
from jax import lax
from jax.experimental import pallas as pl
from jax.experimental.pallas import tpu as pltpu
from jax.sharding import PartitionSpec as P

HD = 128
QB = 128
KB = 64


def dot_nt(a, b):
    return lax.dot_general(a, b, (((1,), (1,)), ((), ())), preferred_element_type=jnp.float32)


def dot_tn(a, b):
    return lax.dot_general(a, b, (((0,), (0,)), ((), ())), preferred_element_type=jnp.float32)


def attend_kernel(heads, bias_ref, live_ref, q_ref, g_ref, kv_ref, out_ref, dq_ref, dkv_ref):
    scaling = HD ** (-0.5)
    width = heads * HD
    bias = bias_ref[0]
    live = live_ref[0]
    for h in range(heads):
        cols = slice(h * HD, (h + 1) * HD)
        vcols = slice(width + h * HD, width + (h + 1) * HD)
        q, g = q_ref[:, cols], g_ref[:, cols]
        k, v = kv_ref[:, cols], kv_ref[:, vcols]
        scores = jnp.where(bias > 0.0, dot_nt(q, k) * scaling, -1e30)
        scores = scores - jnp.max(scores, axis=-1, keepdims=True)
        weights = jnp.exp(scores)
        prob = weights / jnp.sum(weights, axis=-1, keepdims=True)
        prob = jnp.where(live > 0.0, prob, 0.0)
        low = prob.astype(jnp.bfloat16)
        out_ref[:, cols] = jnp.dot(low, v, preferred_element_type=jnp.float32).astype(jnp.bfloat16)
        dprob = dot_nt(g, v)
        row = jnp.sum(prob * dprob, axis=-1, keepdims=True)
        ds = (prob * (dprob - row)).astype(jnp.bfloat16)
        dq_ref[:, cols] = (
            jnp.dot(ds, k, preferred_element_type=jnp.float32) * scaling
        ).astype(jnp.bfloat16)
        for start, part in ((h * HD, dot_tn(ds, q) * scaling), (width + h * HD, dot_tn(low, g))):
            high = part.astype(jnp.bfloat16)
            dkv_ref[:, start : start + HD] = high
            dkv_ref[:, 2 * width + start : 2 * width + start + HD] = (
                part - high.astype(jnp.float32)
            ).astype(jnp.bfloat16)


def attend(queries, cotangent, kv, allowed, live, heads):
    blocks = allowed.shape[0]
    keys = kv.shape[0] // blocks
    width = heads * HD
    row_spec = pl.BlockSpec((QB, width), lambda b: (b, 0))
    kv_spec = pl.BlockSpec((keys, 2 * width), lambda b: (b, 0))
    return pl.pallas_call(
        functools.partial(attend_kernel, heads),
        grid=(blocks,),
        in_specs=[
            pl.BlockSpec((1, 1, keys), lambda b: (b, 0, 0)),
            pl.BlockSpec((1, QB, 1), lambda b: (b, 0, 0)),
            row_spec,
            row_spec,
            kv_spec,
        ],
        out_specs=[row_spec, row_spec, pl.BlockSpec((keys, 4 * width), lambda b: (b, 0))],
        out_shape=[
            jax.ShapeDtypeStruct(queries.shape, jnp.bfloat16),
            jax.ShapeDtypeStruct(queries.shape, jnp.bfloat16),
            jax.ShapeDtypeStruct((kv.shape[0], 4 * width), jnp.bfloat16),
        ],
    )(allowed, live, queries, cotangent, kv)


def per_device(
    video_query, out_grad, audio_latents, kv_weight, video_length, audio_length, align_list
):
    frames = lax.axis_size("frame")
    audio_count = lax.axis_size("audio")
    clip_count = lax.axis_size("dp")
    audio_at = lax.axis_index("audio")
    queries, cotangent, latents = video_query[0], out_grad[0], audio_latents[0]
    shard_rows = queries.shape[0]
    width = queries.shape[1]
    local_width = kv_weight.shape[2]
    heads = local_width // HD
    video_live, audio_live, block_lists = video_length[0], audio_length[0], align_list[0]
    listed_count = block_lists.shape[1]
    own_blocks = shard_rows // QB

    latents_all = lax.all_gather(latents, "audio", axis=0, tiled=True)
    key_count = latents_all.shape[0]
    q = lax.all_to_all(queries, "frame", split_axis=1, concat_axis=0, tiled=True)
    g = lax.all_to_all(cotangent, "frame", split_axis=1, concat_axis=0, tiled=True)

    lists = block_lists.reshape(frames, audio_count, own_blocks, listed_count)
    listed = lax.dynamic_index_in_dim(lists, audio_at, 1, keepdims=False)
    listed = listed.reshape(frames * own_blocks, listed_count)
    block_at = (
        jnp.arange(frames)[:, None] * audio_count + audio_at
    ) * own_blocks + jnp.arange(own_blocks)[None]
    block_at = block_at.reshape(-1)
    key_index = (listed[:, :, None] * KB + jnp.arange(KB)).reshape(
        frames * own_blocks, 1, listed_count * KB
    )
    allowed = (key_index < audio_live).astype(jnp.float32)
    row_index = block_at[:, None] * QB + jnp.arange(QB)[None]
    live = (row_index < video_live).astype(jnp.float32)[:, :, None]

    chosen = jnp.take(
        latents_all.reshape(key_count // KB, KB, width), listed.reshape(-1), axis=0
    ).reshape(-1, width)
    kv = jnp.dot(
        chosen, kv_weight.reshape(width, 2 * local_width), preferred_element_type=jnp.float32
    ).astype(jnp.bfloat16)
    attended, query_grad, terms = attend(q, g, kv, allowed, live, heads)
    terms = lax.all_gather(terms, "audio", axis=0, tiled=True)
    attended = lax.all_to_all(attended, "frame", split_axis=0, concat_axis=1, tiled=True)
    query_grad = lax.all_to_all(query_grad, "frame", split_axis=0, concat_axis=1, tiled=True)

    entries = lists.transpose(1, 0, 2, 3).reshape(-1)
    entry_rows = (entries[:, None] * KB + jnp.arange(KB)[None]).reshape(-1)
    onehot = (jnp.arange(key_count)[:, None] == entry_rows[None]).astype(jnp.bfloat16)
    high, low = terms[:, : 2 * local_width], terms[:, 2 * local_width :]
    kv_grad = (
        jnp.dot(onehot, high, preferred_element_type=jnp.float32)
        + jnp.dot(onehot, low, preferred_element_type=jnp.float32)
    ).astype(jnp.bfloat16)
    weight_rows = width // (clip_count * audio_count)
    columns = lax.dynamic_index_in_dim(
        latents_all.reshape(key_count, clip_count, audio_count, weight_rows),
        audio_at, 2, keepdims=False,
    ).reshape(key_count, clip_count * weight_rows)
    product = dot_tn(columns, kv_grad) * (1.0 / clip_count)
    weight_grad = lax.psum_scatter(
        product.astype(jnp.bfloat16), "dp", scatter_dimension=0, tiled=True
    ).astype(jnp.float32)
    return (attended[None], query_grad[None], weight_grad.reshape(weight_rows, 2, local_width))


def solution(mesh):
    return jax.shard_map(
        per_device,
        mesh=mesh,
        in_specs=(
            P("dp", ("frame", "audio"), None),
            P("dp", ("frame", "audio"), None),
            P("dp", "audio", None),
            P(None, None, "frame"),
            P("dp"),
            P("dp"),
            P("dp", None, None),
        ),
        out_specs=(
            P("dp", ("frame", "audio"), None),
            P("dp", ("frame", "audio"), None),
            P(("dp", "audio"), None, "frame"),
        ),
        check_vma=False,
    )
```

time: 684 us -> 305 us (0.45)
  waiting for transfers between devices: 454 us -> 153 us
  local copies, waits for them, and re-layouts: 96.3 us -> 49.8 us
  other arithmetic: 35 us -> 2.78 us
  matrix products: 67.5 us -> 39.6 us
  Pallas kernels: 0 us -> 18.1 us
  blocking collectives: 0 us -> 13.9 us
    unnamed x4 -> x3, waiting for transfers between devices: 328 us -> 0.71 us
    all_gather x1 -> x2, waiting for transfers between devices: 7.95 us -> 88.4 us  [the longest x1 70.5 us: per_device(): terms = lax.all_gather(terms, 'audio', axis=0, tiled=True)]
    unnamed x24 -> x12, local copies, waits for them, and re-layouts: 64.9 us -> 21.2 us
    reduce_scatter x1, waiting for transfers between devices: 97.3 us -> 55.1 us  [per_device(): lax.psum_scatter(product.astype(jnp.bfloat16), 'dp', scatter_dimension=0,...]
    dot_general x8 -> x3, matrix products: 67.5 us -> 39.6 us  [the longest x1 17 us: dot_tn(): lax.dot_general(a, b, (((0,), (0,)), ((), ())), preferred_element_type=jn...]
    pallas_call x0 -> x1, Pallas kernels: none -> 18.1 us  [attend(): pl.pallas_call(functools.partial(attend_kernel, heads), grid=(blocks,), i...]
    all_to_all x0 -> x1, blocking collectives: none -> 13.9 us  [per_device(): lax.all_to_all(query_grad, 'frame', split_axis=0, concat_axis=1, tiled=True)]
    sub x1 -> x0, other arithmetic: 13.7 us -> none  [softmax_core(): scores = scores - jnp.max(scores, axis=-1, keepdims=True)]
  transfers between devices with their start and end apart: 7 -> 6, of which waited for: 6 -> 5; matrix products, arithmetic and copies ran while one was open for 6% -> 18% of each run, Pallas kernels for 0% -> 0%
where the time goes in v1:
time: 305 us
  waiting for transfers between devices  153 us (50%)
  local copies, waits for them, and re-layouts  49.8 us (16%)
  matrix products  39.6 us (13%)
  Pallas kernels  18.1 us (6%)
  between operations  15.2 us (5%)
  blocking collectives  13.9 us (5%)
  starting transfers between devices  11.8 us (4%)
    all_gather x1, waiting for transfers between devices, per_device(): terms = lax.all_gather(terms, 'audio', axis=0, tiled=True)  70.5 us
    reduce_scatter x1, waiting for transfers between devices, per_device(): lax.psum_scatter(product.astype(jnp.bfloat16), 'dp', scatter_dimension=0,...  55.1 us
    unnamed x12, local copies, waits for them, and re-layouts  21.2 us
    pallas_call x1, Pallas kernels, attend(): pl.pallas_call(functools.partial(attend_kernel, heads), grid=(blocks,), i...  18.1 us
    all_gather x1, waiting for transfers between devices, per_device(): latents_all = lax.all_gather(latents, 'audio', axis=0, tiled=True)  17.9 us
    dot_general x1, matrix products, dot_tn(): lax.dot_general(a, b, (((0,), (0,)), ((), ())), preferred_element_type=jn...  17 us
    all_to_all x1, blocking collectives, per_device(): lax.all_to_all(query_grad, 'frame', split_axis=0, concat_axis=1, tiled=True)  13.9 us
    dot_general x1, matrix products, per_device(): jnp.dot(onehot, high, preferred_element_type=jnp.float32)  12.2 us
  transfers between devices with their start and end apart: 6, of which 5 were waited for; matrix products, arithmetic and copies ran while one was open for 18% of the time, Pallas kernels for 0%

profile of v1, /device:TPU:0, one launch (start us, length us, event | category | flops | bytes accessed | tf_op | source)
XLA Modules:
  0.0 304.5 jit_solution(15526578196800200474)
XLA Ops:
  7.2 0.0 all-gather.6.cloned.1.call-start
  7.2 0.7 all-gather.6.cloned.1.call-update
  7.9 2.6 all_to_all.52
  10.5 1.0 copy.38
  11.5 4.2 %all-to-all-start = ((bf16[128,2,1536]{2,0,1:T(8,128)(2,1)}), bf16[128,2,1536]{2,0,1:T(8,128)(2,1)S(1)}, u32[]{:S(2)}, u32[]{:S(2)}) async-start(bf16[128,2,1536]{2,0,1:T(8,128)(2,1)} %copy.38), calls=%async_computation | async-start | bytes 1572864 | tf_op jit(solution)/shard_map/all_to_all | solution.py:98
  15.7 0.1 reshape_squeeze.3
  15.8 0.1 constant_dynamic-slice_fusion.1
  15.8 0.1 copy.44
  15.9 0.1 reshape_reshape.6
  16.0 0.1 reshape_reshape.5
  17.4 0.1 add.108
  17.5 0.1 add.105
  17.6 0.1 add.106
  17.7 0.6 all_to_all.56
  18.2 1.0 copy.39
  19.2 20.2 %copy.45 = bf16[384,8,2,1536]{3,1,2,0:T(8,128)(2,1)} copy(bf16[384,8,2,1536]{3,2,1,0:T(2,128)(2,1)} %bitcast.37) | data formatting | bytes 37748736
  39.4 0.6 compare_convert_fusion.bias_ref
  40.0 0.7 fusion.14.live_ref
  40.7 17.9 %all-gather.6.cloned.1.call-done = bf16[1,1024,3072]{2,1,0:T(8,128)(2,1)} async-done(((bf16[1,256,3072]{2,1,0:T(8,128)(2,1)}), bf16[1,1024,3072]{2,1,0:T(8,128)(2,1)}) %all-gather.6.cloned.1.call-update) | async-done | bytes 6291472 | tf_op jit(solution)/shard_map/all_gather | solution.py:96
  58.7 3.4 %gather_fusion = bf16[4,64,3072]{2,1,0:T(8,128)(2,1)S(1)} fusion(bf16[16,64,3072]{2,1,0:T(8,128)(2,1)} %bitcast.39, s32[1024]{0:T(1024)S(1)} %pad_clamp_fusion), kind=kCustom, calls=%fused_computation | custom fusion | bytes 3145744 | tf_op jit(solution)/shard_map/jit(_take)/gather | solution.py:115
  62.1 1.4 broadcast_select_fusion
  63.5 3.5 %all-to-all-start.1 = ((bf16[128,2,1536]{2,0,1:T(8,128)(2,1)}), bf16[128,2,1536]{2,0,1:T(8,128)(2,1)S(1)}, u32[]{:S(2)}, u32[]{:S(2)}) async-start(bf16[128,2,1536]{2,0,1:T(8,128)(2,1)} %copy.39), calls=%async_computation.1 | async-start | bytes 1572864 | tf_op jit(solution)/shard_map/all_to_all | solution.py:99
  67.0 0.0 all-gather.4.cloned.1.call-start
  67.1 10.4 %convolution_convert_fusion.kv_ref = bf16[256,3072]{1,0:T(8,128)(2,1)} fusion(bf16[256,3072]{1,0:T(8,128)(2,1)} %bitcast.45, bf16[3072,3072]{1,0:T(8,128)(2,1)} %bitcast.38), kind=kOutput, calls=%fused_computation.9 | convolution fusion | flops 4832624640 | bytes 22020096 | tf_op jit(solution)/shard_map/dot_general | solution.py:118
  77.4 1.0 all-to-all-done.1
  78.5 0.9 copy-done.1
  79.4 18.1 %shard_map.94 = (bf16[256,1536]{1,0:T(8,128)(2,1)}, bf16[256,1536]{1,0:T(8,128)(2,1)}, bf16[256,6144]{1,0:T(8,128)(2,1)}) custom-call(f32[2,1,128]{2,1,0:T(1,128)} %compare_convert_fusion.bias_ref, f32[2,128,1]{2,1,0:T(8,128)} %fusion.14.live_ref, bf16[256,1536]{1,0:T(8,128)(2,1)} %bitcast.43, bf16[256,1536]{1,0:T(8,128)(2,1)} %bitcast.44, ...), custom_call_target="tpu_custom_call" | custom-call | tf_op jit(solution)/shard_map/pallas_call | solution.py:61
  97.5 0.0 all-gather.4.cloned.1.call-update
  97.5 0.2 reduce-scatter.2.cloned.1.call-start
  97.7 0.1 copy.43
  97.8 0.1 mul.53
  97.9 0.1 iota_add_fusion
  98.0 0.1 add.121
  98.1 8.8 %copy.42 = bf16[1,1024,3072]{1,2,0:T(8,128)(2,1)} copy(bf16[1,1024,3072]{2,1,0:T(8,128)(2,1)} %all-gather.6.cloned.1.call-done) | data formatting | bytes 12582912 | tf_op jit(solution)/shard_map/all_gather | solution.py:96
  106.8 1.9 constant_dynamic-slice_fusion
  108.7 70.5 %all-gather.4.cloned.1.call-done = bf16[1024,6144]{1,0:T(8,128)(2,1)} async-done(((bf16[256,6144]{1,0:T(8,128)(2,1)}), bf16[1024,6144]{1,0:T(8,128)(2,1)}) %all-gather.4.cloned.1.call-update) | async-done | bytes 12582928 | tf_op jit(solution)/shard_map/all_gather | solution.py:122
  179.2 12.2 %fusion.7 = f32[1024,3072]{1,0:T(8,128)} fusion(bf16[1024,6144]{1,0:T(8,128)(2,1)} %all-gather.4.cloned.1.call-done, s32[1024]{0:T(1024)S(1)} %add.121), kind=kOutput, calls=%fused_computation.6 | convolution fusion | flops 6443499520 | bytes 18878464 | tf_op jit(solution)/shard_map/dot_general | solution.py:131
  191.4 17.0 %multiply_convert_fusion = bf16[768,3072]{1,0:T(8,128)(2,1)} fusion(bf16[1024,768]{0,1:T(8,128)(2,1)S(1)} %bitcast.46, f32[1024,3072]{1,0:T(8,128)} %fusion.7, bf16[1024,6144]{1,0:T(8,128)(2,1)} %all-gather.4.cloned.1.call-done, s32[1024]{0:T(1024)S(1)} %add.121), kind=kOutput, calls=%fused_computation.2 | convolution fusion | flops 11286347776 | bytes 25169920 | tf_op jit(solution)/shard_map/dot_general | solution.py:21
  208.4 0.0 reduce-scatter.2.cloned.1.call-update
  208.4 13.9 %all_to_all.70 = bf16[2,128,1536]{2,1,0:T(8,128)(2,1)S(1)} all-to-all(bf16[2,128,1536]{2,1,0:T(8,128)(2,1)S(1)} %bitcast.47), channel_id=1, replica_groups=mesh['dp'=4,'frame'=2,'audio'=4] {'frame'}, dimensions={0} | all-to-all | bytes 1572864 | tf_op jit(solution)/shard_map/all_to_all | solution.py:124
  222.3 3.8 %all-to-all-start.2 = ((bf16[2,128,1536]{2,1,0:T(8,128)(2,1)}), bf16[2,128,1536]{2,1,0:T(8,128)(2,1)S(1)}, u32[]{:S(2)}, u32[]{:S(2)}) async-start(bf16[2,128,1536]{2,1,0:T(8,128)(2,1)} %bitcast.10), calls=%async_computation.2 | async-start | bytes 1572864 | tf_op jit(solution)/shard_map/all_to_all | solution.py:123
  226.1 0.8 copy.41
  226.9 1.5 broadcast_in_dim.25
  228.4 8.1 %all-to-all-done.2 = bf16[2,128,1536]{2,1,0:T(8,128)(2,1)S(1)} async-done(((bf16[2,128,1536]{2,1,0:T(8,128)(2,1)}), bf16[2,128,1536]{2,1,0:T(8,128)(2,1)S(1)}, u32[]{:S(2)}, u32[]{:S(2)}) %all-to-all-start.2) | async-done | bytes 786464 | tf_op jit(solution)/shard_map/all_to_all | solution.py:123
  236.5 0.8 copy.40
  237.3 1.5 broadcast_in_dim.24
  238.8 55.1 %reduce-scatter.2.cloned.1.call-done = bf16[192,3072]{1,0:T(8,128)(2,1)} async-done(((bf16[768,3072]{1,0:T(8,128)(2,1)}), bf16[192,3072]{1,0:T(8,128)(2,1)}) %reduce-scatter.2.cloned.1.call-update) | async-done | bytes 1179664 | tf_op jit(solution)/shard_map/reduce_scatter | solution.py:140
  293.9 4.1 %reshape.244 = f32[192,2,1536]{2,1,0:T(2,128)} reshape(bf16[192,3072]{1,0:T(8,128)(2,1)} %reduce-scatter.2.cloned.1.call-done) | data formatting | bytes 3538944 | tf_op jit(solution)/shard_map/reshape | solution.py:143
  (17 shorter events, 0.1 us)
Async XLA Ops:
  7.2 8.5 %copy-start.4 = (s32[1,8,2]{1,2,0:T(2,128)S(1)}, s32[1,8,2]{1,2,0:T(2,128)}, u32[]{:S(2)}) copy-start(s32[1,8,2]{1,2,0:T(2,128)} %param.13) | copy-start | bytes 196
  7.2 10.5 %copy-start.2 = (bf16[1,128,3072]{2,1,0:T(8,128)(2,1)S(1)}, bf16[1,128,3072]{2,1,0:T(8,128)(2,1)}, u32[]{:S(2)}) copy-start(bf16[1,128,3072]{2,1,0:T(8,128)(2,1)} %param.8) | copy-start | bytes 2359300
  7.2 51.5 %all-gather.6.cloned.1.call-start = ((), (), s32[]{:S(2)}) async-start(), calls=%async_computation.7 | async-start | bytes 7864320 | tf_op jit(solution)/shard_map/all_gather | solution.py:96
  11.5 52.0 %all-to-all-start = ((bf16[128,2,1536]{2,0,1:T(8,128)(2,1)}), bf16[128,2,1536]{2,0,1:T(8,128)(2,1)S(1)}, u32[]{:S(2)}, u32[]{:S(2)}) async-start(bf16[128,2,1536]{2,0,1:T(8,128)(2,1)} %copy.38), calls=%async_computation | async-start | bytes 1572864 | tf_op jit(solution)/shard_map/all_to_all | solution.py:98
  63.5 14.0 %copy-start = (bf16[128,2,1536]{2,0,1:T(8,128)(2,1)}, bf16[128,2,1536]{2,0,1:T(8,128)(2,1)S(1)}, u32[]{:S(2)}) copy-start(bf16[128,2,1536]{2,0,1:T(8,128)(2,1)S(1)} %all-to-all-done) | copy-start | bytes 2359300
  63.5 15.0 %all-to-all-start.1 = ((bf16[128,2,1536]{2,0,1:T(8,128)(2,1)}), bf16[128,2,1536]{2,0,1:T(8,128)(2,1)S(1)}, u32[]{:S(2)}, u32[]{:S(2)}) async-start(bf16[128,2,1536]{2,0,1:T(8,128)(2,1)} %copy.39), calls=%async_computation.1 | async-start | bytes 1572864 | tf_op jit(solution)/shard_map/all_to_all | solution.py:99
  67.0 112.2 %all-gather.4.cloned.1.call-start = ((), (), s32[]{:S(2)}) async-start(), calls=%async_computation.5 | async-start | bytes 15728640 | tf_op jit(solution)/shard_map/all_gather | solution.py:122
  78.5 0.9 copy-start.1
  97.5 196.4 %reduce-scatter.2.cloned.1.call-start = ((), (), s32[]{:S(2)}) async-start(), calls=%async_computation.6 | async-start | bytes 5898240 | tf_op jit(solution)/shard_map/reduce_scatter | solution.py:140
  191.4 17.0 %copy-start.3 = (bf16[256,1536]{1,0:T(8,128)(2,1)S(1)}, bf16[256,1536]{1,0:T(8,128)(2,1)}, u32[]{:S(2)}) copy-start(bf16[256,1536]{1,0:T(8,128)(2,1)} %get-tuple-element.7) | copy-start | bytes 2359300
  222.3 14.2 %all-to-all-start.2 = ((bf16[2,128,1536]{2,1,0:T(8,128)(2,1)}), bf16[2,128,1536]{2,1,0:T(8,128)(2,1)S(1)}, u32[]{:S(2)}, u32[]{:S(2)}) async-start(bf16[2,128,1536]{2,1,0:T(8,128)(2,1)} %bitcast.10), calls=%async_computation.2 | async-start | bytes 1572864 | tf_op jit(solution)/shard_map/all_to_all | solution.py:123
Sparse Core Ops, SparseCore 0:
  9.6 49.0 all-gather.5
  97.6 81.5 all-gather.3
  208.6 85.2 reduce-scatter.1

commit v2 on v1

--- a/solution.py
+++ b/solution.py
@@ -21,7 +21,7 @@
     return lax.dot_general(a, b, (((0,), (0,)), ((), ())), preferred_element_type=jnp.float32)
 
 
-def attend_kernel(heads, bias_ref, live_ref, q_ref, g_ref, kv_ref, out_ref, dq_ref, dkv_ref):
+def attend_kernel(heads, chunk, bias_ref, live_ref, q_ref, g_ref, kv_ref, out_ref, dq_ref, dkv_ref):
     scaling = HD ** (-0.5)
     width = heads * HD
     bias = bias_ref[0]
@@ -46,8 +46,9 @@
         ).astype(jnp.bfloat16)
         for start, part in ((h * HD, dot_tn(ds, q) * scaling), (width + h * HD, dot_tn(low, g))):
             high = part.astype(jnp.bfloat16)
-            dkv_ref[:, start : start + HD] = high
-            dkv_ref[:, 2 * width + start : 2 * width + start + HD] = (
+            at, lane = divmod(start, chunk)
+            dkv_ref[at, :, lane : lane + HD] = high
+            dkv_ref[at, :, chunk + lane : chunk + lane + HD] = (
                 part - high.astype(jnp.float32)
             ).astype(jnp.bfloat16)
 
@@ -56,10 +57,12 @@
     blocks = allowed.shape[0]
     keys = kv.shape[0] // blocks
     width = heads * HD
+    chunk = math.gcd(2 * width, 512)
+    chunks = 2 * width // chunk
     row_spec = pl.BlockSpec((QB, width), lambda b: (b, 0))
     kv_spec = pl.BlockSpec((keys, 2 * width), lambda b: (b, 0))
     return pl.pallas_call(
-        functools.partial(attend_kernel, heads),
+        functools.partial(attend_kernel, heads, chunk),
         grid=(blocks,),
         in_specs=[
             pl.BlockSpec((1, 1, keys), lambda b: (b, 0, 0)),
@@ -68,13 +71,249 @@
             row_spec,
             kv_spec,
         ],
-        out_specs=[row_spec, row_spec, pl.BlockSpec((keys, 4 * width), lambda b: (b, 0))],
+        out_specs=[row_spec, row_spec, pl.BlockSpec((chunks, keys, 2 * chunk), lambda b: (0, b, 0))],
         out_shape=[
             jax.ShapeDtypeStruct(queries.shape, jnp.bfloat16),
             jax.ShapeDtypeStruct(queries.shape, jnp.bfloat16),
-            jax.ShapeDtypeStruct((kv.shape[0], 4 * width), jnp.bfloat16),
+            jax.ShapeDtypeStruct((chunks, kv.shape[0], 2 * chunk), jnp.bfloat16),
         ],
     )(allowed, live, queries, cotangent, kv)
+
+
+MESH = pl.DeviceIdType.MESH
+
+
+def grad_kernel(
+    axes, chunk, terms_ref, att_ref, dq_ref, onehot_ref, latents_ref,
+    out_ref, att_out, dq_out,
+    latents_vmem, cols_t, gathered, kv_tile, partial, right_buf, left_buf,
+    local_sem, own_sem, far_send, far_recv, near_send, near_recv, fwd_send, fwd_recv,
+    right_send, right_recv, left_send, left_recv, ret_send, ret_recv,
+):
+    clips, frames, audio = axes
+    z, f, a = lax.axis_index("dp"), lax.axis_index("frame"), lax.axis_index("audio")
+    chunks = terms_ref.shape[0]
+    rows = terms_ref.shape[1]
+    weight_rows = out_ref.shape[1]
+    key_count = onehot_ref.shape[0]
+    lane = att_ref.shape[2]
+    half = audio // 2
+    far = lax.rem(a + half, audio)
+    near = a + 1 - 2 * lax.rem(a, 2)
+    far_near = lax.rem(near + half, audio)
+
+    load = pltpu.make_async_copy(latents_ref, latents_vmem, local_sem)
+    load.start()
+
+    barrier = pltpu.get_barrier_semaphore()
+
+    def greet(where):
+        pl.semaphore_signal(barrier, inc=1, device_id=where, device_id_type=MESH)
+
+    greet({"audio": far})
+    greet({"audio": near})
+    for step in range(1, frames):
+        greet({"frame": lax.rem(f + step, frames)})
+    pl.when(z > 0)(lambda: greet({"dp": z - 1}))
+    pl.when(z < clips - 1)(lambda: greet({"dp": z + 1}))
+    ends = jnp.where(z > 0, 1, 0) + jnp.where(z < clips - 1, 1, 0)
+    pl.semaphore_wait(barrier, 1 + frames + ends)
+
+    def far_copy(c):
+        return pltpu.make_async_remote_copy(
+            src_ref=terms_ref.at[c], dst_ref=gathered.at[c, a], send_sem=far_send.at[c],
+            recv_sem=far_recv.at[c], device_id={"audio": far}, device_id_type=MESH)
+
+    def near_copy(c):
+        return pltpu.make_async_remote_copy(
+            src_ref=terms_ref.at[c], dst_ref=gathered.at[c, a], send_sem=near_send.at[c],
+            recv_sem=near_recv.at[c], device_id={"audio": near}, device_id_type=MESH)
+
+    def fwd_copy(c):
+        return pltpu.make_async_remote_copy(
+            src_ref=gathered.at[c, far], dst_ref=gathered.at[c, far], send_sem=fwd_send.at[c],
+            recv_sem=fwd_recv.at[c], device_id={"audio": near}, device_id_type=MESH)
+
+    def arrived(c, source, sem, peer):
+        return pltpu.make_async_remote_copy(
+            src_ref=terms_ref.at[c], dst_ref=gathered.at[c, source], send_sem=far_send.at[c],
+            recv_sem=sem.at[c], device_id={"audio": peer}, device_id_type=MESH)
+
+    def own_copy(c):
+        return pltpu.make_async_copy(terms_ref.at[c], gathered.at[c, a], own_sem.at[c])
+
+    def issue(c, carry):
+        far_copy(c).start()
+        near_copy(c).start()
+        own_copy(c).start()
+        return carry
+
+    lax.fori_loop(0, chunks, issue, 0)
+
+    def lanes(g):
+        return pl.ds(pl.multiple_of(g * lane, 128), lane)
+
+    def returns(step):
+        other = lax.rem(f + step, frames)
+        return [
+            pltpu.make_async_remote_copy(
+                src_ref=src.at[other], dst_ref=dst.at[:, lanes(f)],
+                send_sem=ret_send.at[which, step], recv_sem=ret_recv.at[which, step],
+                device_id={"frame": other}, device_id_type=MESH)
+            for which, (src, dst) in enumerate(((att_ref, att_out), (dq_ref, dq_out)))
+        ]
+
+    for step in range(1, frames):
+        for copy in returns(step):
+            copy.start()
+    att_out[:, lanes(f)] = att_ref[f]
+    dq_out[:, lanes(f)] = dq_ref[f]
+
+    load.wait()
+    width = latents_vmem.shape[1]
+
+    def select(d, carry):
+        first = (d * audio + a) * weight_rows
+        at = lax.broadcasted_iota(jnp.int32, (weight_rows, width), 1)
+        row = lax.broadcasted_iota(jnp.int32, (weight_rows, width), 0)
+        pick = jnp.where(at == row + first, 1.0, 0.0).astype(jnp.bfloat16)
+        cols_t[d] = dot_nt(pick, latents_vmem[...]).astype(jnp.bfloat16)
+        return carry
+
+    lax.fori_loop(0, clips, select, 0)
+
+    tile = math.gcd(key_count, 256)
+
+    def compute(c):
+        own_copy(c).wait()
+        arrived(c, far, far_recv, far).wait_recv()
+        fwd_copy(c).start()
+        arrived(c, near, near_recv, near).wait_recv()
+        arrived(c, far_near, fwd_recv, near).wait_recv()
+
+        def dedupe(t, carry):
+            at = pl.ds(pl.multiple_of(t * tile, tile), tile)
+            total = jnp.zeros((tile, chunk), jnp.float32)
+            for source in range(audio):
+                pick = onehot_ref[at, source * rows : (source + 1) * rows]
+                total += jnp.dot(
+                    pick, gathered[c, source, :, :chunk], preferred_element_type=jnp.float32)
+                total += jnp.dot(
+                    pick, gathered[c, source, :, chunk:], preferred_element_type=jnp.float32)
+            kv_tile[at, :] = total.astype(jnp.bfloat16)
+            return carry
+
+        lax.fori_loop(0, key_count // tile, dedupe, 0)
+
+        def multiply(d, carry):
+            partial[c, d] = jnp.dot(
+                cols_t[d], kv_tile[...], preferred_element_type=jnp.float32
+            ) * (1.0 / clips)
+            return carry
+
+        lax.fori_loop(0, clips, multiply, 0)
+        out_ref[c] = partial[c, z]
+
+    def hop(buf, send, recv, c, d, where):
+        return pltpu.make_async_remote_copy(
+            src_ref=buf.at[c, d], dst_ref=buf.at[c, d], send_sem=send.at[c, d],
+            recv_sem=recv.at[c, d], device_id={"dp": where}, device_id_type=MESH)
+
+    def pass_on(c, forward):
+        if forward:
+            buf, send, recv, peer, source = right_buf, right_send, right_recv, z + 1, z - 1
+            has_source = z > 0
+        else:
+            buf, send, recv, peer, source = left_buf, left_send, left_recv, z - 1, z + 1
+            has_source = z < clips - 1
+        for d in range(clips):
+            @pl.when((d > z) if forward else (d < z))
+            def _():
+                @pl.when(has_source)
+                def _():
+                    hop(buf, send, recv, c, d, source).wait_recv()
+                    buf[c, d] = (partial[c, d] + buf[c, d].astype(jnp.float32)).astype(jnp.bfloat16)
+
+                @pl.when(jnp.logical_not(has_source))
+                def _():
+                    buf[c, d] = partial[c, d].astype(jnp.bfloat16)
+
+                hop(buf, send, recv, c, d, peer).start()
+
+        @pl.when(has_source)
+        def _():
+            hop(buf, send, recv, c, z, source).wait_recv()
+            out_ref[c] += buf[c, z].astype(jnp.float32)
+
+    def advance(i, carry):
+        pl.when(i < chunks)(lambda: compute(i))
+        for forward, lag in ((True, z), (False, clips - 1 - z)):
+            c = i - lag
+
+            @pl.when(jnp.logical_and(c >= 0, c < chunks))
+            def _():
+                pass_on(c, forward)
+
+        return carry
+
+    lax.fori_loop(0, chunks + clips - 1, advance, 0)
+
+    def drain(c, carry):
+        far_copy(c).wait_send()
+        near_copy(c).wait_send()
+        fwd_copy(c).wait_send()
+        for d in range(clips):
+            pl.when(d > z)(lambda: hop(right_buf, right_send, right_recv, c, d, z + 1).wait_send())
+            pl.when(d < z)(lambda: hop(left_buf, left_send, left_recv, c, d, z - 1).wait_send())
+        return carry
+
+    lax.fori_loop(0, chunks, drain, 0)
+    for step in range(1, frames):
+        for copy in returns(step):
+            copy.wait_send()
+        source = lax.rem(f + frames - step, frames)
+        for which, (src, dst) in enumerate(((att_ref, att_out), (dq_ref, dq_out))):
+            pltpu.make_async_remote_copy(
+                src_ref=src.at[source], dst_ref=dst.at[:, lanes(source)],
+                send_sem=ret_send.at[which, step], recv_sem=ret_recv.at[which, step],
+                device_id={"frame": source}, device_id_type=MESH).wait_recv()
+
+
+def finish(terms, attended, query_grad, onehot, latents_all, sizes, weight_rows):
+    clips, frames, audio = sizes
+    chunks, rows, pair = terms.shape
+    chunk = pair // 2
+    own_rows, lane = attended.shape[1], attended.shape[2]
+    key_count = onehot.shape[0]
+    vmem = pl.BlockSpec(memory_space=pltpu.VMEM)
+    dma = pltpu.SemaphoreType.DMA
+    line = (chunks, clips)
+    kernel = functools.partial(grad_kernel, sizes, chunk)
+    return pl.pallas_call(
+        kernel,
+        in_specs=[vmem] * 4 + [pl.BlockSpec(memory_space=pl.ANY)],
+        out_specs=[vmem] * 3,
+        out_shape=[
+            jax.ShapeDtypeStruct((chunks, weight_rows, chunk), jnp.float32),
+            jax.ShapeDtypeStruct((own_rows, frames * lane), jnp.bfloat16),
+            jax.ShapeDtypeStruct((own_rows, frames * lane), jnp.bfloat16),
+        ],
+        scratch_shapes=[
+            pltpu.VMEM(latents_all.shape, jnp.bfloat16),
+            pltpu.VMEM((clips, weight_rows, key_count), jnp.bfloat16),
+            pltpu.VMEM((chunks, audio, rows, pair), jnp.bfloat16),
+            pltpu.VMEM((key_count, chunk), jnp.bfloat16),
+            pltpu.VMEM((chunks, clips, weight_rows, chunk), jnp.float32),
+            pltpu.VMEM((chunks, clips, weight_rows, chunk), jnp.bfloat16),
+            pltpu.VMEM((chunks, clips, weight_rows, chunk), jnp.bfloat16),
+            dma, dma((chunks,)), dma((chunks,)), dma((chunks,)), dma((chunks,)),
+            dma((chunks,)), dma((chunks,)), dma((chunks,)),
+            dma(line), dma(line), dma(line), dma(line),
+            dma((2, frames)), dma((2, frames)),
+        ],
+        compiler_params=pltpu.CompilerParams(
+            collective_id=0, has_side_effects=True, vmem_limit_bytes=66_000_000),
+    )(terms, attended, query_grad, onehot, latents_all)
 
 
 def per_device(
@@ -119,28 +358,21 @@
         chosen, kv_weight.reshape(width, 2 * local_width), preferred_element_type=jnp.float32
     ).astype(jnp.bfloat16)
     attended, query_grad, terms = attend(q, g, kv, allowed, live, heads)
-    terms = lax.all_gather(terms, "audio", axis=0, tiled=True)
-    attended = lax.all_to_all(attended, "frame", split_axis=0, concat_axis=1, tiled=True)
-    query_grad = lax.all_to_all(query_grad, "frame", split_axis=0, concat_axis=1, tiled=True)
-
     entries = lists.transpose(1, 0, 2, 3).reshape(-1)
     entry_rows = (entries[:, None] * KB + jnp.arange(KB)[None]).reshape(-1)
     onehot = (jnp.arange(key_count)[:, None] == entry_rows[None]).astype(jnp.bfloat16)
-    high, low = terms[:, : 2 * local_width], terms[:, 2 * local_width :]
-    kv_grad = (
-        jnp.dot(onehot, high, preferred_element_type=jnp.float32)
-        + jnp.dot(onehot, low, preferred_element_type=jnp.float32)
-    ).astype(jnp.bfloat16)
     weight_rows = width // (clip_count * audio_count)
-    columns = lax.dynamic_index_in_dim(
-        latents_all.reshape(key_count, clip_count, audio_count, weight_rows),
-        audio_at, 2, keepdims=False,
-    ).reshape(key_count, clip_count * weight_rows)
-    product = dot_tn(columns, kv_grad) * (1.0 / clip_count)
-    weight_grad = lax.psum_scatter(
-        product.astype(jnp.bfloat16), "dp", scatter_dimension=0, tiled=True
-    ).astype(jnp.float32)
-    return (attended[None], query_grad[None], weight_grad.reshape(weight_rows, 2, local_width))
+    weight_grad, attended, query_grad = finish(
+        terms,
+        attended.reshape(frames, shard_rows, local_width),
+        query_grad.reshape(frames, shard_rows, local_width),
+        onehot,
+        latents_all,
+        (clip_count, frames, audio_count),
+        weight_rows,
+    )
+    weight_grad = weight_grad.transpose(1, 0, 2).reshape(weight_rows, 2, local_width)
+    return (attended[None], query_grad[None], weight_grad)
 
 
 def solution(mesh):

time: 305 us -> 227 us (0.74)
  waiting for transfers between devices: 153 us -> 18.8 us
  Pallas kernels: 18.1 us -> 131 us
  matrix products: 39.6 us -> 10.4 us
  blocking collectives: 13.9 us -> 0 us
  local copies, waits for them, and re-layouts: 49.8 us -> 37.8 us
  starting transfers between devices: 11.8 us -> 7.81 us
    pallas_call x1 -> x2, Pallas kernels: 18.1 us -> 131 us  [the longest x1 113 us: finish(): pl.pallas_call(kernel, in_specs=[vmem] * 4 + [pl.BlockSpec(memory_space=p...]
    all_gather x1 -> x0, waiting for transfers between devices: 70.5 us -> none  [per_device(): terms = lax.all_gather(terms, 'audio', axis=0, tiled=True)]
    reduce_scatter x1 -> x0, waiting for transfers between devices: 55.1 us -> none  [per_device(): lax.psum_scatter(product.astype(jnp.bfloat16), 'dp', scatter_dimension=0,...]
    dot_general x2 -> x0, matrix products: 29.2 us -> none  [the longest x1 17 us: dot_tn(): lax.dot_general(a, b, (((0,), (0,)), ((), ())), preferred_element_type=jn...]
    all_to_all x1 -> x0, blocking collectives: 13.9 us -> none  [per_device(): lax.all_to_all(query_grad, 'frame', split_axis=0, concat_axis=1, tiled=True)]
    all_gather x1 -> x0, local copies, waits for them, and re-layouts: 8.77 us -> none  [per_device(): latents_all = lax.all_gather(latents, 'audio', axis=0, tiled=True)]
    all_to_all x1 -> x0, waiting for transfers between devices: 8.1 us -> none  [per_device(): lax.all_to_all(attended, 'frame', split_axis=0, concat_axis=1, tiled=True)]
    all_to_all x1 -> x0, starting transfers between devices: 3.77 us -> none  [per_device(): lax.all_to_all(attended, 'frame', split_axis=0, concat_axis=1, tiled=True)]
  transfers between devices with their start and end apart: 6 -> 3, of which waited for: 5 -> 2; matrix products, arithmetic and copies ran while one was open for 18% -> 18% of each run, Pallas kernels for 0% -> 0%
where the time goes in v2:
time: 227 us
  Pallas kernels  131 us (58%)
  local copies, waits for them, and re-layouts  37.8 us (17%)
  waiting for transfers between devices  18.8 us (8%)
  between operations  15.4 us (7%)
  matrix products  10.4 us (5%)
  starting transfers between devices  7.81 us (3%)
  other arithmetic  4.95 us (2%)
    pallas_call x1, Pallas kernels, finish(): pl.pallas_call(kernel, in_specs=[vmem] * 4 + [pl.BlockSpec(memory_space=p...  113 us
    unnamed x16, local copies, waits for them, and re-layouts  24.5 us
    pallas_call x1, Pallas kernels, attend(): pl.pallas_call(functools.partial(attend_kernel, heads, chunk), grid=(bloc...  18.1 us
    all_gather x1, waiting for transfers between devices, per_device(): latents_all = lax.all_gather(latents, 'audio', axis=0, tiled=True)  17.1 us
    dot_general x1, matrix products, per_device(): jnp.dot(chosen, kv_weight.reshape(width, 2 * local_width), preferred_elem...  10.4 us
  transfers between devices with their start and end apart: 3, of which 2 were waited for; matrix products, arithmetic and copies ran while one was open for 18% of the time, Pallas kernels for 0%

profile of v2, /device:TPU:0, one launch (start us, length us, event | category | flops | bytes accessed | tf_op | source)
XLA Modules:
  0.0 226.6 jit_solution(9149052145381832078)
XLA Ops:
  7.2 0.0 copy-start.2
  7.2 0.0 all-gather.3.cloned.1.call-start
  7.2 0.7 all-gather.3.cloned.1.call-update
  7.9 0.4 copy-done.2
  8.3 0.0 copy-start.5
  8.3 0.6 all_to_all.28
  8.9 1.0 copy.25
  9.8 4.2 %all-to-all-start = ((bf16[128,2,1536]{2,0,1:T(8,128)(2,1)}), bf16[128,2,1536]{2,0,1:T(8,128)(2,1)S(1)}, u32[]{:S(2)}, u32[]{:S(2)}) async-start(bf16[128,2,1536]{2,0,1:T(8,128)(2,1)} %copy.25), calls=%async_computation | async-start | bytes 1572864 | tf_op jit(solution)/shard_map/all_to_all | solution.py:337
  14.1 0.0 copy-done.5
  14.1 0.1 reshape_squeeze.3
  14.2 0.1 constant_dynamic-slice_fusion
  14.2 0.1 copy.29
  14.3 0.1 reshape_reshape.6
  14.4 0.1 reshape_reshape.5
  14.5 0.0 copy-start.3
  14.5 20.1 %copy.30 = bf16[384,8,2,1536]{3,1,2,0:T(8,128)(2,1)} copy(bf16[384,8,2,1536]{3,2,1,0:T(2,128)(2,1)} %bitcast.36) | data formatting | bytes 37748736
  34.6 0.1 add.98
  34.7 0.1 add.99
  34.8 0.1 add.101
  36.2 0.0 copy-done.3
  36.2 0.6 all_to_all.32
  36.8 1.0 copy.26
  37.7 0.1 copy.27
  37.8 0.1 mul.47
  37.9 0.1 iota_add_fusion
  38.0 0.1 add.114
  38.1 0.5 compare_convert_fusion.bias_ref
  38.6 0.7 fusion.1.live_ref
  39.4 2.2 fusion.onehot_ref
  41.6 17.1 %all-gather.3.cloned.1.call-done = bf16[1,1024,3072]{2,1,0:T(8,128)(2,1)} async-done(((bf16[1,256,3072]{2,1,0:T(8,128)(2,1)}), bf16[1,1024,3072]{2,1,0:T(8,128)(2,1)}) %all-gather.3.cloned.1.call-update) | async-done | bytes 6291472 | tf_op jit(solution)/shard_map/all_gather | solution.py:335
  58.7 3.4 %gather_fusion = bf16[4,64,3072]{2,1,0:T(8,128)(2,1)S(1)} fusion(bf16[16,64,3072]{2,1,0:T(8,128)(2,1)} %bitcast.38, s32[1024]{0:T(1024)S(1)} %pad_clamp_fusion), kind=kCustom, calls=%fused_computation | custom fusion | bytes 3145744 | tf_op jit(solution)/shard_map/jit(_take)/gather | solution.py:354
  62.1 1.4 broadcast_select_fusion
  63.5 0.0 all-to-all-done
  63.5 0.0 copy-start
  63.5 3.5 %all-to-all-start.1 = ((bf16[128,2,1536]{2,0,1:T(8,128)(2,1)}), bf16[128,2,1536]{2,0,1:T(8,128)(2,1)S(1)}, u32[]{:S(2)}, u32[]{:S(2)}) async-start(bf16[128,2,1536]{2,0,1:T(8,128)(2,1)} %copy.26), calls=%async_computation.1 | async-start | bytes 1572864 | tf_op jit(solution)/shard_map/all_to_all | solution.py:338
  67.0 10.4 %convolution_convert_fusion.kv_ref = bf16[256,3072]{1,0:T(8,128)(2,1)} fusion(bf16[256,3072]{1,0:T(8,128)(2,1)} %bitcast.43, bf16[3072,3072]{1,0:T(8,128)(2,1)} %bitcast.37), kind=kOutput, calls=%fused_computation.3 | convolution fusion | flops 4832624640 | bytes 22020096 | tf_op jit(solution)/shard_map/dot_general | solution.py:357
  77.4 0.0 copy-done
  77.4 1.1 all-to-all-done.1
  78.5 0.0 copy-start.1
  78.5 0.9 copy-done.1
  79.3 18.1 %shard_map.94 = (bf16[256,1536]{1,0:T(8,128)(2,1)}, bf16[256,1536]{1,0:T(8,128)(2,1)}, bf16[6,256,1024]{2,1,0:T(8,128)(2,1)}) custom-call(f32[2,1,128]{2,1,0:T(1,128)} %compare_convert_fusion.bias_ref, f32[2,128,1]{2,1,0:T(8,128)} %fusion.1.live_ref, bf16[256,1536]{1,0:T(8,128)(2,1)} %bitcast.40, bf16[256,1536]{1,0:T(8,128)(2,1)} %bitcast.41, ...), custom_call_target="tpu_custom_call" | custom-call | tf_op jit(solution)/shard_map/pallas_call | solution.py:64
  97.5 113.3 %shard_map.95 = (f32[6,192,512]{2,1,0:T(8,128)}, bf16[128,3072]{1,0:T(8,128)(2,1)}, bf16[128,3072]{1,0:T(8,128)(2,1)}) custom-call(bf16[6,256,1024]{2,1,0:T(8,128)(2,1)} %get-tuple-element.9.terms_ref, bf16[2,128,1536]{2,1,0:T(8,128)(2,1)} %bitcast.44, bf16[2,128,1536]{2,1,0:T(8,128)(2,1)} %bitcast.45, bf16[1024,1024]{1,0:T(8,128)(2,1)} %fusion.onehot_ref, ...), custom_call_target="tpu_custom_call" | custom-call | tf_op jit(solution)/shard_map/pallas_call | solution.py:292
  210.8 3.1 %copy.28 = f32[192,6,512]{2,1,0:T(8,128)S(1)} copy(f32[192,6,512]{2,0,1:T(8,128)} %bitcast.42) | data formatting | bytes 4718592 | tf_op jit(solution)/shard_map/transpose | solution.py:374
  213.9 2.8 %reshape.229 = f32[192,2,1536]{2,1,0:T(2,128)} reshape(f32[192,6,512]{2,1,0:T(8,128)S(1)} %copy.28) | data formatting | bytes 4718592 | tf_op jit(solution)/shard_map/reshape | solution.py:374
  216.8 0.0 copy-start.4
  216.8 2.1 copy.35
  218.9 0.0 copy-done.4
  218.9 0.9 copy.36
  (7 shorter events, 0.0 us)
Async XLA Ops:
  7.2 1.1 copy-start.2
  7.2 51.5 %all-gather.3.cloned.1.call-start = ((), (), s32[]{:S(2)}) async-start(), calls=%async_computation.2 | async-start | bytes 7864320 | tf_op jit(solution)/shard_map/all_gather | solution.py:335
  8.3 5.8 %copy-start.5 = (s32[1,8,2]{1,2,0:T(2,128)S(1)}, s32[1,8,2]{1,2,0:T(2,128)}, u32[]{:S(2)}) copy-start(s32[1,8,2]{1,2,0:T(2,128)} %param.13) | copy-start | bytes 196
  9.8 53.6 %all-to-all-start = ((bf16[128,2,1536]{2,0,1:T(8,128)(2,1)}), bf16[128,2,1536]{2,0,1:T(8,128)(2,1)S(1)}, u32[]{:S(2)}, u32[]{:S(2)}) async-start(bf16[128,2,1536]{2,0,1:T(8,128)(2,1)} %copy.25), calls=%async_computation | async-start | bytes 1572864 | tf_op jit(solution)/shard_map/all_to_all | solution.py:337
  14.5 21.7 %copy-start.3 = (bf16[1,128,3072]{2,1,0:T(8,128)(2,1)S(1)}, bf16[1,128,3072]{2,1,0:T(8,128)(2,1)}, u32[]{:S(2)}) copy-start(bf16[1,128,3072]{2,1,0:T(8,128)(2,1)} %param.8) | copy-start | bytes 2359300
  63.5 13.9 %copy-start = (bf16[128,2,1536]{2,0,1:T(8,128)(2,1)}, bf16[128,2,1536]{2,0,1:T(8,128)(2,1)S(1)}, u32[]{:S(2)}) copy-start(bf16[128,2,1536]{2,0,1:T(8,128)(2,1)S(1)} %all-to-all-done) | copy-start | bytes 2359300
  63.5 15.0 %all-to-all-start.1 = ((bf16[128,2,1536]{2,0,1:T(8,128)(2,1)}), bf16[128,2,1536]{2,0,1:T(8,128)(2,1)S(1)}, u32[]{:S(2)}, u32[]{:S(2)}) async-start(bf16[128,2,1536]{2,0,1:T(8,128)(2,1)} %copy.26), calls=%async_computation.1 | async-start | bytes 1572864 | tf_op jit(solution)/shard_map/all_to_all | solution.py:338
  78.5 0.9 copy-start.1
  216.8 2.1 copy-start.4
Sparse Core Ops, SparseCore 0:
  9.5 49.0 all-gather.2
